TPU v7x, 512 devices: a whole 4x4x16 slice. The times are simulated.
512 devices in a mesh: outer: 8 (over x, y_lo), inner: 64 (over z, y_hi, core).
Axes of the slice: x: 4, y: 4 (y_hi: 2, y_lo: 2; y = y_hi * 2 + y_lo), z: 16, core: 2. Of those that a mesh axis runs over, the one named last changes fastest.
Arguments:
- queries: bfloat16 [16384, 2048], P('inner'), may hold values from -128 to 128
- mem_keys: bfloat16 [8192, 2048], P(('outer', 'inner')), may hold values from -4.5 to 4.5
- mem_values: bfloat16 [8192, 2048], P(('outer', 'inner')), may hold values from -6 to 6
Outputs:
- attended: bfloat16 [16384, 2048], P('inner')
- log_total: float32 [16384, 16], P('inner')
All inputs are finite; a program needn't handle non-finite values.
Results may differ from a plain program's by a relative error of at most 0.014.
Values may be sent and summed in bfloat16 or wider, within the bound.
No kernel may reach another device: no remote copies, remote signals or barrier semaphores. Data moves between devices by JAX's collectives and lax.ppermute only.
A program may use at most 64 MiB of HBM per device.

v0:
```python
import math

import jax
import jax.numpy as jnp
from jax import lax
from jax.sharding import PartitionSpec as P

HEADS = 16
HEAD_DIM = 128


def on_device(queries, mem_keys, mem_values):
    row_count = queries.shape[0]
    columns = queries.shape[1]
    scale = 1.0 / math.sqrt(HEAD_DIM)
    query_heads = queries.reshape(row_count, HEADS, HEAD_DIM)
    initial = (
        jnp.full((row_count, HEADS), -jnp.inf, jnp.float32),
        jnp.zeros((row_count, HEADS), jnp.float32),
        jnp.zeros((row_count, HEADS, HEAD_DIM), jnp.float32),
    )
    key_piece = lax.all_gather(mem_keys, "inner", axis=0, tiled=True)
    value_piece = lax.all_gather(mem_values, "inner", axis=0, tiled=True)
    entries = key_piece.shape[0]
    block = math.gcd(entries, 256)
    key_blocks = key_piece.reshape(entries // block, block, HEADS, HEAD_DIM)
    value_blocks = value_piece.reshape(entries // block, block, HEADS, HEAD_DIM)

    def one_block(running, blocks):
        running_top, running_total, running_out = running
        key_block, value_block = blocks
        scores = (
            jnp.einsum("thd,khd->thk", query_heads, key_block, preferred_element_type=jnp.float32)
            * scale
        )
        new_top = jnp.maximum(running_top, jnp.max(scores, axis=-1))
        fading = jnp.exp(running_top - new_top)
        raw = jnp.exp(scores - new_top[..., None])
        new_total = running_total * fading + jnp.sum(raw, axis=-1)
        product = jnp.einsum(
            "thk,khd->thd",
            raw.astype(jnp.bfloat16),
            value_block,
            preferred_element_type=jnp.float32,
        )
        new_out = running_out * fading[..., None] + product
        return ((new_top, new_total, new_out), None)

    result, unused = lax.scan(one_block, initial, (key_blocks, value_blocks))
    group_peak, group_total, group_out = result
    peak = lax.pmax(group_peak, "outer")
    factor = jnp.exp(group_peak - peak)
    weighted = (group_out * factor[..., None]).reshape(row_count, columns)
    total = lax.psum(group_total * factor, "outer")
    log_total = peak + jnp.log(total)
    summed = lax.psum(weighted.astype(jnp.bfloat16), "outer").astype(jnp.float32)
    attended = (
        (summed.reshape(row_count, HEADS, HEAD_DIM) / total[..., None])
        .astype(jnp.bfloat16)
        .reshape(row_count, columns)
    )
    return (attended, log_total)


def solution(mesh):
    in_specs = (P("inner", None), P(("outer", "inner"), None), P(("outer", "inner"), None))
    out_specs = (P("inner", None), P("inner", None))
    return jax.shard_map(
        on_device, mesh=mesh, in_specs=in_specs, out_specs=out_specs, check_vma=False
    )
```

profile of v0, /device:TPU:32, one launch (start us, length us, event | category | flops | bytes accessed | tf_op | source)
XLA Modules:
  0.0 486.1 jit_solution(9600157572781027679)
XLA Ops:
  8.7 1.5 copy.9
  10.2 1.3 copy.11
  11.5 154.5 %all-gather.3.cloned.1.call-done = bf16[1024,2048]{1,0:T(8,128)(2,1)} async-done(((bf16[16,2048]{1,0:T(8,128)(2,1)}), bf16[1024,2048]{1,0:T(8,128)(2,1)}) %all-gather.3.cloned.1.call-update) | async-done | bytes 4194320 | tf_op jit(solution)/shard_map/all_gather | solution.py:22
  166.0 5.5 %copy.19 = bf16[128,8,16,128]{3,2,1,0:T(8,128)(2,1)} copy(bf16[128,8,16,128]{3,1,2,0:T(8,128)(2,1)} %bitcast.54) | data formatting | bytes 8388608
  171.6 142.9 %all-gather.5.cloned.1.call-done = bf16[1024,2048]{1,0:T(8,128)(2,1)} async-done(((bf16[16,2048]{1,0:T(8,128)(2,1)}), bf16[1024,2048]{1,0:T(8,128)(2,1)}) %all-gather.5.cloned.1.call-update) | async-done | bytes 4194320 | tf_op jit(solution)/shard_map/all_gather | solution.py:23
  314.4 5.6 %copy.20 = bf16[128,8,16,128]{3,2,1,0:T(8,128)(2,1)} copy(bf16[128,8,16,128]{3,1,2,0:T(8,128)(2,1)} %bitcast.55) | data formatting | bytes 8388608
  320.0 33.2 %while.15 = (s32[]{:T(128)}, f32[256,16]{0,1:T(8,128)S(1)}, f32[256,16]{0,1:T(8,128)S(1)}, f32[256,16,128]{0,2,1:T(8,128)}, bf16[4,256,16,128]{3,2,1,0:T(8,128)(...) while((s32[]{:T(128)}, f32[256,16]{0,1:T(8,128)S(1)}, ...), condition=%wide.region_3.4_spmd.clone, body=%wide.region_0.3_spmd.clone.sunk | while | flops 546852864 | bytes 43253932 | solution.py:49
  320.0 1.9 constant_dynamic-slice_fusion.3
  321.9 0.8 copy.30
  322.7 2.1 bitcast_reduce_fusion.2
  325.6 1.4 bitcast_add_fusion.2
  327.0 1.3 copy-done.1
  328.3 1.9 constant_dynamic-slice_fusion.3
  330.2 0.8 copy.30
  331.0 2.1 bitcast_reduce_fusion.2
  333.9 1.4 bitcast_add_fusion.2
  335.3 1.3 copy-done.1
  336.6 1.9 constant_dynamic-slice_fusion.3
  338.5 0.8 copy.30
  339.3 2.1 bitcast_reduce_fusion.2
  342.2 1.4 bitcast_add_fusion.2
  343.6 1.3 copy-done.1
  344.9 1.9 constant_dynamic-slice_fusion.3
  347.6 2.1 bitcast_reduce_fusion.2
  350.5 1.4 bitcast_add_fusion.2
  351.9 1.3 copy-done.1
  353.2 33.2 %pmax.7 = f32[256,16]{0,1:T(8,128)S(1)} all-reduce(f32[256,16]{0,1:T(8,128)S(1)} %get-tuple-element.42), channel_id=1, replica_groups=mesh['outer'=8,'inner'=64] {'outer'}, use_global_device_ids=true, to_apply=%region_4.5 | all-reduce | flops 4096 | bytes 32768 | tf_op jit(solution)/shard_map/pmax | solution.py:51
  386.4 1.8 multiply_convert_fusion
  388.2 1.4 copy.16
  389.6 31.2 %psum.15 = f32[256,16]{0,1:T(8,128)S(1)} all-reduce(f32[256,16]{0,1:T(8,128)S(1)} %get-tuple-element.91), channel_id=1, replica_groups=mesh['outer'=8,'inner'=64] {'outer'}, use_global_device_ids=true, to_apply=%region_6.7 | all-reduce | flops 4096 | bytes 32768 | tf_op jit(solution)/shard_map/psum | solution.py:54
  421.6 54.3 %all-reduce.2.cloned.1.call-done = bf16[256,2048]{1,0:T(8,128)(2,1)} async-done(((bf16[256,2048]{1,0:T(8,128)(2,1)}), bf16[256,2048]{1,0:T(8,128)(2,1)}) %all-reduce.2.cloned.1.call-update) | async-done | bytes 1048592 | tf_op jit(solution)/shard_map/psum | solution.py:56
  476.5 3.1 fusion.13
  (42 shorter events, 6.6 us)
Async XLA Ops:
  7.2 158.9 %all-gather.3.cloned.1.call-start = ((), (), s32[]{:S(2)}) async-start(), calls=%async_computation | async-start | bytes 4259840 | tf_op jit(solution)/shard_map/all_gather | solution.py:22
  7.9 306.5 %all-gather.5.cloned.1.call-start = ((), (), s32[]{:S(2)}) async-start(), calls=%async_computation.1 | async-start | bytes 4259840 | tf_op jit(solution)/shard_map/all_gather | solution.py:23
  8.6 467.2 %all-reduce.2.cloned.1.call-start = ((), (), s32[]{:S(2)}) async-start(), calls=%async_computation.2 | async-start | bytes 2097152 | tf_op jit(solution)/shard_map/psum | solution.py:56
  322.7 2.9 copy-start
  326.9 1.3 copy-start.1
  331.0 2.9 copy-start
  335.2 1.3 copy-start.1
  339.3 2.9 copy-start
  343.5 1.3 copy-start.1
  347.6 2.9 copy-start
  351.8 1.3 copy-start.1
Sparse Core Ops, SparseCore 0:
  11.3 154.7 all-gather.2
  169.3 145.0 all-gather.4
  389.7 86.0 all-reduce.1
where the time goes:
time: 487 us; the launch traced here: 486 us
  waiting for transfers between devices  353 us (72%)
  blocking collectives  64.4 us (13%)
  local copies, waits for them, and re-layouts  32.1 us (7%)
  matrix products  13.9 us (3%)
  between operations  13.8 us (3%)
  other arithmetic  8.47 us (2%)
    all_gather x1, waiting for transfers between devices, on_device(): key_piece = lax.all_gather(mem_keys, 'inner', axis=0, tiled=True)  154 us
    all_gather x1, waiting for transfers between devices, on_device(): value_piece = lax.all_gather(mem_values, 'inner', axis=0, tiled=True)  143 us
    psum x1, waiting for transfers between devices, on_device(): lax.psum(weighted.astype(jnp.bfloat16), 'outer').astype(jnp.float32)  54.3 us
    pmax x1, blocking collectives, on_device(): peak = lax.pmax(group_peak, 'outer')  33.2 us
    psum x1, blocking collectives, on_device(): total = lax.psum(group_total * factor, 'outer')  31.2 us
    unnamed x4, local copies, waits for them, and re-layouts  13.9 us
    dynamic_slice x8, local copies, waits for them, and re-layouts, on_device(): result, unused = lax.scan(one_block, initial, (key_blocks, value_blocks))  10.8 us
  transfers between devices with their start and end apart: 3, of which 3 were waited for; matrix products, arithmetic and copies ran while one was open for 2% of the time, Pallas kernels for 0%

commit v1 on v0

v1 whole, which is shorter than its diff:
```python
import functools
import math

import jax
import jax.numpy as jnp
from jax import lax
from jax.experimental import pallas as pl
from jax.experimental.pallas import tpu as pltpu
from jax.sharding import Mesh
from jax.sharding import PartitionSpec as P

HEADS = 16
DIM = 128
SCALE = 1.0 / math.sqrt(DIM)
TO_BASE_TWO = SCALE / math.log(2.0)

NAMES = ("x", "y_lo", "z", "y_hi", "core")
SIZES = (4, 2, 16, 2, 2)
OUTER = ("x", "y_lo")
INNER = ("z", "y_hi", "core")
PLANE = ("x", "y_lo", "y_hi")

OWN = 16
SHARE = 32
PEERS = 16
LINE = OWN * PEERS
TOKENS = SHARE * PEERS

VMEM = pltpu.VMEM


def whole(count):
    return [pl.BlockSpec(memory_space=VMEM)] * count


def pack_kernel(which, q_ref, k_ref, v_ref, out_ref):
    for head in range(HEADS):
        columns = slice(head * DIM, (head + 1) * DIM)
        out_ref[head, 0:OWN, :] = k_ref[:, columns]
        out_ref[head, OWN : 2 * OWN, :] = v_ref[:, columns]
        out_ref[head, 2 * OWN : 2 * OWN + SHARE, :] = q_ref[:, columns]


def pack(which, queries, keys, values):
    columns = HEADS * DIM
    grid_spec = pltpu.PrefetchScalarGridSpec(
        num_scalar_prefetch=1,
        grid=(1,),
        in_specs=[
            pl.BlockSpec((SHARE, columns), lambda i, w: (w[0], 0)),
            pl.BlockSpec((OWN, columns), lambda i, w: (0, 0)),
            pl.BlockSpec((OWN, columns), lambda i, w: (0, 0)),
        ],
        out_specs=pl.BlockSpec((HEADS, 2 * OWN + SHARE, DIM), lambda i, w: (0, 0, 0)),
    )
    return pl.pallas_call(
        pack_kernel,
        out_shape=jax.ShapeDtypeStruct((HEADS, 2 * OWN + SHARE, DIM), jnp.bfloat16),
        grid_spec=grid_spec,
        name="pack",
    )(which, queries, keys, values)


def spread_kernel(in_ref, kv_ref, q_ref):
    for peer in range(PEERS):
        for source in range(PEERS):
            rows = slice(source * OWN, (source + 1) * OWN)
            kv_ref[peer, rows, :] = in_ref[source, 0:OWN, :]
        for source in range(PEERS):
            rows = slice(LINE + source * OWN, LINE + (source + 1) * OWN)
            kv_ref[peer, rows, :] = in_ref[source, OWN : 2 * OWN, :]
    for source in range(PEERS):
        q_ref[source * SHARE : (source + 1) * SHARE, :] = in_ref[source, 2 * OWN :, :]


def spread(received):
    return pl.pallas_call(
        spread_kernel,
        out_shape=(
            jax.ShapeDtypeStruct((PEERS, 2 * LINE, DIM), jnp.bfloat16),
            jax.ShapeDtypeStruct((TOKENS, DIM), jnp.bfloat16),
        ),
        in_specs=whole(1),
        out_specs=tuple(whole(2)),
        name="spread",
    )(received)


T_BLOCK = 256
P_BLOCK = 4


def attend(q, kv_ref, first, state):
    keys = kv_ref[first : first + P_BLOCK, 0:LINE, :].reshape(P_BLOCK * LINE, DIM)
    values = kv_ref[first : first + P_BLOCK, LINE:, :].reshape(P_BLOCK * LINE, DIM)
    scores = lax.dot_general(
        q, keys, (((1,), (1,)), ((), ())), preferred_element_type=jnp.float32
    )
    top = jnp.max(scores, axis=1, keepdims=True)
    if state is not None:
        top = jnp.maximum(top, state[0])
    raw = jnp.exp2((scores - top) * TO_BASE_TWO)
    total = jnp.sum(raw, axis=1, keepdims=True)
    out = jnp.dot(raw.astype(jnp.bfloat16), values, preferred_element_type=jnp.float32)
    if state is not None:
        fading = jnp.exp2((state[0] - top) * TO_BASE_TWO)
        total = total + state[1] * fading
        out = out + state[2] * fading
    return top, total, out


def first_kernel(q_ref, kv_ref, top_ref, total_ref, out_ref):
    for block in range(TOKENS // T_BLOCK):
        rows = slice(block * T_BLOCK, (block + 1) * T_BLOCK)
        q = q_ref[rows, :]
        state = None
        for first in range(0, PEERS, P_BLOCK):
            state = attend(q, kv_ref, first, state)
        top_ref[rows, :] = jnp.broadcast_to(state[0], (T_BLOCK, DIM))
        total_ref[rows, :] = jnp.broadcast_to(state[1], (T_BLOCK, DIM))
        out_ref[rows, :] = state[2]


def second_kernel(q_ref, kv_ref, top_ref, total_ref, out_ref, packed_ref):
    for block in range(TOKENS // T_BLOCK):
        rows = slice(block * T_BLOCK, (block + 1) * T_BLOCK)
        q = q_ref[rows, :]
        state = (top_ref[rows, 0:1], total_ref[rows, 0:1], out_ref[rows, :])
        for first in range(0, PEERS, P_BLOCK):
            state = attend(q, kv_ref, first, state)
        top, total, out = state
        packed_ref[rows, 0:DIM] = (out / total).astype(jnp.bfloat16)
        log_total = top * SCALE + jnp.log(total)
        high = log_total.astype(jnp.bfloat16)
        low = (log_total - high.astype(jnp.float32)).astype(jnp.bfloat16)
        lane = lax.broadcasted_iota(jnp.int32, (T_BLOCK, DIM), 1)
        packed_ref[rows, DIM:] = jnp.where(
            lane < HEADS, high.astype(jnp.float32), low.astype(jnp.float32)
        ).astype(jnp.bfloat16)


COST = pl.CostEstimate(
    flops=4 * TOKENS * PEERS * LINE * DIM,
    bytes_accessed=2 * PEERS * 2 * LINE * DIM,
    transcendentals=TOKENS * PEERS * LINE,
)


def flash_first(q, kv):
    return pl.pallas_call(
        first_kernel,
        out_shape=(jax.ShapeDtypeStruct((TOKENS, DIM), jnp.float32),) * 3,
        in_specs=whole(2),
        out_specs=tuple(whole(3)),
        cost_estimate=COST,
        name="first_half",
    )(q, kv)


def flash_second(q, kv, state):
    return pl.pallas_call(
        second_kernel,
        out_shape=jax.ShapeDtypeStruct((TOKENS, 2 * DIM), jnp.bfloat16),
        in_specs=whole(5),
        out_specs=whole(1)[0],
        cost_estimate=COST,
        name="second_half",
    )(q, kv, *state)


N_OUTER = 8
WIDE = HEADS * DIM + DIM


def gather_kernel(in_ref, out_ref):
    lane = lax.broadcasted_iota(jnp.int32, (SHARE, DIM), 1)
    logs = jnp.zeros((SHARE, DIM), jnp.float32)
    for head in range(HEADS):
        here = in_ref[head, :, DIM:].astype(jnp.float32)
        logs = jnp.where((lane == head) | (lane == HEADS + head), here, logs)
    logs = logs.astype(jnp.bfloat16)
    for copy in range(N_OUTER):
        for head in range(HEADS):
            out_ref[copy, :, head * DIM : (head + 1) * DIM] = in_ref[head, :, 0:DIM]
        out_ref[copy, :, HEADS * DIM :] = logs


def widen(received):
    return pl.pallas_call(
        gather_kernel,
        out_shape=jax.ShapeDtypeStruct((N_OUTER, SHARE, WIDE), jnp.bfloat16),
        in_specs=whole(1),
        out_specs=whole(1)[0],
        name="widen",
    )(received)


def finish_kernel(in_ref, attended_ref, log_ref):
    for source in range(N_OUTER):
        rows = slice(source * SHARE, (source + 1) * SHARE)
        attended_ref[rows, :] = in_ref[source, :, 0 : HEADS * DIM]
        logs = in_ref[source, :, HEADS * DIM :].astype(jnp.float32)
        log_ref[rows, :] = logs[:, 0:HEADS] + logs[:, HEADS : 2 * HEADS]


def finish(received):
    rows = N_OUTER * SHARE
    return pl.pallas_call(
        finish_kernel,
        out_shape=(
            jax.ShapeDtypeStruct((rows, HEADS * DIM), jnp.bfloat16),
            jax.ShapeDtypeStruct((rows, HEADS), jnp.float32),
        ),
        in_specs=whole(1),
        out_specs=tuple(whole(2)),
        name="finish",
    )(received)


def on_device(queries, mem_keys, mem_values):
    which = lax.axis_index(OUTER).astype(jnp.int32).reshape(1)
    packed = pack(which, queries, mem_keys, mem_values)
    received = lax.all_to_all(packed, "z", 0, 0)
    spread_out, q = spread(received)
    own = lax.all_to_all(spread_out, PLANE, 0, 0)
    other = lax.ppermute(own, "core", [(0, 1), (1, 0)])
    state = flash_first(q, own)
    result = flash_second(q, other, state)
    back = lax.all_to_all(result.reshape(PEERS, SHARE, 2 * DIM), "z", 0, 0)
    full = lax.all_to_all(widen(back), OUTER, 0, 0)
    return finish(full)


def solution(mesh):
    named = Mesh(mesh.devices.reshape(SIZES), NAMES)
    in_specs = (P(INNER, None), P(OUTER + INNER, None), P(OUTER + INNER, None))
    out_specs = (P(INNER, None), P(INNER, None))
    return jax.shard_map(
        on_device, mesh=named, in_specs=in_specs, out_specs=out_specs, check_vma=False
    )
```

time: 487 us -> 141 us (0.29)
  waiting for transfers between devices: 353 us -> 0.01 us
  blocking collectives: 64.4 us -> 114 us
  local copies, waits for them, and re-layouts: 32.1 us -> 1.58 us
  Pallas kernels: 0 us -> 22.4 us
  matrix products: 13.9 us -> 0 us
  between operations: 13.8 us -> 0.66 us
  other arithmetic: 8.47 us -> 0 us
    all_gather x2 -> x0, waiting for transfers between devices: 297 us -> none  [the longest x1 154 us: on_device(): key_piece = lax.all_gather(mem_keys, 'inner', axis=0, tiled=True)]
    all_to_all x0 -> x4, blocking collectives: none -> 114 us  [the longest x1 34.5 us: on_device(): own = lax.all_to_all(spread_out, PLANE, 0, 0)]
    psum x1 -> x0, waiting for transfers between devices: 54.3 us -> none  [on_device(): lax.psum(weighted.astype(jnp.bfloat16), 'outer').astype(jnp.float32)]
    pmax x1 -> x0, blocking collectives: 33.2 us -> none  [on_device(): peak = lax.pmax(group_peak, 'outer')]
    psum x1 -> x0, blocking collectives: 31.2 us -> none  [on_device(): total = lax.psum(group_total * factor, 'outer')]
    pallas_call x0 -> x6, Pallas kernels: none -> 22.4 us  [the longest x1 7.38 us: flash_second(): pl.pallas_call(second_kernel, out_shape=jax.ShapeDtypeStruct((TOKENS, 2 *...]
    unnamed x4 -> x2, local copies, waits for them, and re-layouts: 13.9 us -> 0.01 us
    dot_general x8 -> x0, matrix products: 13.9 us -> none  [the longest x4 8.4 us: one_block(): jnp.einsum('thd,khd->thk', query_heads, key_block, preferred_element_type...]
  transfers between devices with their start and end apart: 3 -> 1, of which waited for: 3 -> 0; matrix products, arithmetic and copies ran while one was open for 2% -> 0% of each run, Pallas kernels for 0% -> 5%
where the time goes in v1:
time: 141 us
  blocking collectives  114 us (81%)
  Pallas kernels  22.4 us (16%)
  starting transfers between devices  1.91 us (1%)
  local copies, waits for them, and re-layouts  1.58 us (1%)
    all_to_all x1, blocking collectives, on_device(): own = lax.all_to_all(spread_out, PLANE, 0, 0)  34.5 us
    all_to_all x1, blocking collectives, on_device(): received = lax.all_to_all(packed, 'z', 0, 0)  33.2 us
    all_to_all x1, blocking collectives, on_device(): back = lax.all_to_all(result.reshape(PEERS, SHARE, 2 * DIM), 'z', 0, 0)  26.1 us
    all_to_all x1, blocking collectives, on_device(): full = lax.all_to_all(widen(back), OUTER, 0, 0)  20.4 us
    pallas_call x1, Pallas kernels, flash_second(): pl.pallas_call(second_kernel, out_shape=jax.ShapeDtypeStruct((TOKENS, 2 *...  7.38 us
    pallas_call x1, Pallas kernels, flash_first(): pl.pallas_call(first_kernel, out_shape=(jax.ShapeDtypeStruct((TOKENS, DIM...  6.36 us
  transfers between devices with their start and end apart: 1, of which 0 were waited for; matrix products, arithmetic and copies ran while one was open for 0% of the time, Pallas kernels for 5%

profile of v1, /device:TPU:32, one launch (start us, length us, event | category | flops | bytes accessed | tf_op | source)
XLA Modules:
  0.0 140.8 jit_solution(14274558825007437737)
XLA Ops:
  0.6 1.7 %pack.1 = bf16[16,64,128]{2,1,0:T(8,128)(2,1)} custom-call(s32[1]{0:T(128)} %bitcast.which, bf16[256,2048]{1,0:T(8,128)(2,1)} %q_ref.1, bf16[16,2048]{1,0:T(8,128)(2,1)} %k_ref.1, bf16[16,2048]{1,0:T(8,128)(2,1)} %v_ref.1), custom_call_target="tpu_custom_call" | custom-call | tf_op jit(solution)/shard_map/pack/pallas_call | solution.py:56
  2.3 33.2 %all_to_all.20.in_ref = bf16[16,64,128]{2,1,0:T(8,128)(2,1)} all-to-all(bf16[16,64,128]{2,1,0:T(8,128)(2,1)} %pack.1), channel_id=1, replica_groups=mesh['x'=4,'y_lo'=2,'z'=16,'y_hi'=2,'core'=2] {'z'}, dimensions={0} | all-to-all | bytes 524288 | tf_op jit(solution)/shard_map/all_to_all | solution.py:223
  35.5 2.6 %spread.1 = (bf16[16,512,128]{2,1,0:T(8,128)(2,1)}, bf16[512,128]{1,0:T(8,128)(2,1)}) custom-call(bf16[16,64,128]{2,1,0:T(8,128)(2,1)} %all_to_all.20.in_ref), custom_call_target="tpu_custom_call" | custom-call | tf_op jit(solution)/shard_map/spread/pallas_call | solution.py:77
  38.1 34.5 %all_to_all.21.kv_ref = bf16[16,512,128]{2,1,0:T(8,128)(2,1)S(1)} all-to-all(bf16[16,512,128]{2,1,0:T(8,128)(2,1)} %get-tuple-element.8), channel_id=1, replica_groups=mesh['x'=4,'y_lo'=2,'z'=16,'y_hi'=2,'core'=2] {'x','y_lo','y_hi'}, dimensions={0} | all-to-all | bytes 4194304 | tf_op jit(solution)/shard_map/all_to_all | solution.py:225
  72.7 0.0 copy-start
  72.7 1.9 %collective-permute-start = (bf16[16,512,128]{2,1,0:T(8,128)(2,1)S(1)}, bf16[16,512,128]{2,1,0:T(8,128)(2,1)}, u32[]{:S(2)}, u32[]{:S(2)}) collective-permute-start(bf16[16,512,128]{2,1,0:T(8,128)(2,1)S(1)} %all_to_all.21.kv_ref), channel_id=1, source_target_pairs={{0,1},{1,0},{2,3},{3,2},{4,5},{5,4},{6,7},{7,6},{8,9},{9,8},{10,11... | collective-permute-start | bytes 6291464 | tf_op jit(solution)/shard_map/ppermute | solution.py:226
  74.6 0.0 copy-done
  74.6 6.4 %first_half.1 = (f32[512,128]{1,0:T(8,128)}, f32[512,128]{1,0:T(8,128)}, f32[512,128]{1,0:T(8,128)}) custom-call(bf16[512,128]{1,0:T(8,128)(2,1)} %get-tuple-element.7.q_ref, bf16[16,512,128]{2,1,0:T(8,128)(2,1)} %copy-done), custom_call_target="tpu_custom_call" | custom-call | flops 1073741824 | bytes 2097152 | tf_op jit(solution)/shard_map/first_half/pallas_call | solution.py:150
  81.0 0.0 collective-permute-done.kv_ref
  81.0 7.4 %second_half.1 = bf16[512,256]{1,0:T(8,128)(2,1)} custom-call(bf16[512,128]{1,0:T(8,128)(2,1)} %get-tuple-element.7.q_ref, bf16[16,512,128]{2,1,0:T(8,128)(2,1)} %collective-permute-done.kv_ref, f32[512,128]{1,0:T(8,128)} %get-tuple-element.9.top_ref, f32[512,128]{1,0:T(8,128)} %get-tuple-element.10.total_ref, f32[512,128]{1,0:T(8,128)} %get-tuple-element.11.out_ref), custom_call_target="tpu_custom_call" | custom-call | flops 1073741824 | bytes 2097152 | tf_op jit(solution)/shard_map/second_half/pallas_call | solution.py:161
  88.3 26.1 %all_to_all.22.in_ref = bf16[16,32,256]{2,1,0:T(8,128)(2,1)} all-to-all(bf16[16,32,256]{2,1,0:T(8,128)(2,1)} %bitcast.2), channel_id=1, replica_groups=mesh['x'=4,'y_lo'=2,'z'=16,'y_hi'=2,'core'=2] {'z'}, dimensions={0} | all-to-all | bytes 524288 | tf_op jit(solution)/shard_map/all_to_all | solution.py:229
  114.5 2.1 %widen.1 = bf16[8,32,2176]{2,1,0:T(8,128)(2,1)} custom-call(bf16[16,32,256]{2,1,0:T(8,128)(2,1)} %all_to_all.22.in_ref), custom_call_target="tpu_custom_call" | custom-call | tf_op jit(solution)/shard_map/widen/pallas_call | solution.py:189
  116.5 20.4 %all_to_all.23.in_ref = bf16[8,32,2176]{2,1,0:T(8,128)(2,1)} all-to-all(bf16[8,32,2176]{2,1,0:T(8,128)(2,1)} %widen.1), channel_id=1, replica_groups=mesh['x'=4,'y_lo'=2,'z'=16,'y_hi'=2,'core'=2] {'x','y_lo'}, dimensions={0} | all-to-all | bytes 2228224 | tf_op jit(solution)/shard_map/all_to_all | solution.py:230
  136.9 2.3 %finish.1 = (bf16[256,2048]{1,0:T(8,128)(2,1)}, f32[256,16]{1,0:T(8,128)}) custom-call(bf16[8,32,2176]{2,1,0:T(8,128)(2,1)} %all_to_all.23.in_ref), custom_call_target="tpu_custom_call" | custom-call | tf_op jit(solution)/shard_map/finish/pallas_call | solution.py:208
  139.2 1.6 %copy.5 = f32[256,16]{0,1:T(8,128)} copy(f32[256,16]{1,0:T(8,128)} %get-tuple-element.13) | data formatting | bytes 32768 | tf_op jit(solution)/shard_map/finish/pallas_call | solution.py:208
Async XLA Ops:
  72.7 1.9 %copy-start = (bf16[16,512,128]{2,1,0:T(8,128)(2,1)}, bf16[16,512,128]{2,1,0:T(8,128)(2,1)S(1)}, u32[]{:S(2)}) copy-start(bf16[16,512,128]{2,1,0:T(8,128)(2,1)S(1)} %all_to_all.21.kv_ref) | copy-start | bytes 6291460
  72.7 8.3 %collective-permute-start = (bf16[16,512,128]{2,1,0:T(8,128)(2,1)S(1)}, bf16[16,512,128]{2,1,0:T(8,128)(2,1)}, u32[]{:S(2)}, u32[]{:S(2)}) collective-permute-start(bf16[16,512,128]{2,1,0:T(8,128)(2,1)S(1)} %all_to_all.21.kv_ref), channel_id=1, source_target_pairs={{0,1},{1,0},{2,3},{3,2},{4,5},{5,4},{6,7},{7,6},{8,9},{9,8},{10,11... | collective-permute-start | bytes 6291464 | tf_op jit(solution)/shard_map/ppermute | solution.py:226
